TPU v7x, 128 devices: a whole 4x4x4 slice. The times are simulated.
128 devices in a mesh: row: 8 (over y, core), col: 16 (over z, x).
Axes of the slice: x: 4, y: 4, z: 4, core: 2. Of those that a mesh axis runs over, the one named last changes fastest.
Arguments:
- points: float32 [3, 262144], P(None, ('row', 'col')), as said below
- values: float32 [16, 262144], P(None, ('row', 'col'))
- tile_lists: int32 [3, 6144], P(None, ('row', 'col')), may hold values from 0 to 127, as said below
Outputs:
- solution: float32 [16, 262144], P(None, ('row', 'col'))
- residual: float32 [16, 262144], P(None, ('row', 'col'))
Inputs may be any that keep to these rules, and one draw needn't show every extreme that they name: `tile_lists`: on every device the live slots come first and the rest hold 0, 0, 0; a device holds at most 48 live slots and some device holds exactly that many; no unordered pair of blocks is listed twice, in either order. Block pairs whose points can come within the support radius are listed. Coordinates of point blocks that lie in cells of a square lattice of unit cells, 256 points to a block.
All inputs are finite; a program needn't handle non-finite values.
Results may differ from a plain program's by a relative error of at most 0.0003.
Values sent between devices are 32-bit elements; how exact they have to be, the bound alone decides.
A program may use at most 64 MiB of HBM per device.

v0:
```python
import jax
import jax.numpy as jnp
from jax import lax
from jax.experimental import pallas as pl
from jax.experimental.pallas import tpu as pltpu
from jax.sharding import PartitionSpec as P

BLK = 256
MESH = pl.DeviceIdType.MESH
F32 = jnp.float32
BF16 = jnp.bfloat16
VM = pl.BlockSpec(memory_space=pltpu.VMEM)
SM = pl.BlockSpec(memory_space=pltpu.SMEM)


def position():
    nr, nc = lax.axis_size("row"), lax.axis_size("col")
    return lax.axis_index("row"), lax.axis_index("col"), nr, nc


def barrier():
    r, c, nr, nc = position()
    sem = pltpu.get_barrier_semaphore()
    for o in range(1, nc):
        pl.semaphore_signal(sem, 1, device_id=(r, lax.rem(c + o, nc)), device_id_type=MESH)
    for o in range(1, nr):
        pl.semaphore_signal(sem, 1, device_id=(lax.rem(r + o, nr), c), device_id_type=MESH)
    pl.semaphore_wait(sem, nr + nc - 2)


def remote(src, dst, sems, k, to):
    return pltpu.make_async_remote_copy(
        src_ref=src, dst_ref=dst, send_sem=sems.at[0, k], recv_sem=sems.at[1, k],
        device_id=to, device_id_type=MESH,
    )


class Mover:
    def __init__(self, sems):
        self.sems, self.copies = sems, []

    def send(self, src, dst, to):
        copy = remote(src, dst, self.sems, len(self.copies), to)
        copy.start()
        self.copies.append(copy)
        return copy

    def drain(self):
        for copy in self.copies:
            copy.wait_send()


def plane(half):
    r, c, nr, nc = position()
    z, x = lax.div(c, SIDE), lax.rem(c, SIDE)
    first, second = (z, x) if half == 0 else (x, z)

    def slot(df, dg):
        f, g = lax.rem(first + df, SIDE), lax.rem(second + dg, SIDE)
        return f * SIDE + g if half == 0 else g * SIDE + f

    return slot


def column(dy, dcore):
    r, c, nr, nc = position()
    y, core = lax.div(r, 2), lax.rem(r, 2)
    return lax.rem(y + dy, SIDE) * 2 + lax.rem(core + dcore, 2)


HALF = 8
SIDE = 4
WAYS = ((1, 3, 0), (3, 1, 1))


def spread(src, by_row, by_col, sems):
    r, c, nr, nc = position()
    mover = Mover(sems)
    owned = src.shape[1]
    part = owned // 2
    row_to = lambda slot: (r, slot)
    col_to = lambda slot: (slot, c)

    def cell(half, slot, side=None):
        rows = pl.ds(half * HALF, HALF)
        if side is None:
            return by_row.at[slot, rows, :]
        return by_row.at[slot, rows, pl.ds(side * part, part)]

    slots = [plane(0), plane(1)]
    near, far, cross, away = {}, {}, {}, {}
    own = [src.at[pl.ds(half * HALF, HALF), :] for half in (0, 1)]
    for half in (0, 1):
        at = slots[half]
        for go, come, side in WAYS:
            near[half, side] = mover.send(own[half], cell(half, at(0, 0)), row_to(at(go, 0)))
    ring, pair = {}, []
    for go, come, side in WAYS:
        ring[side] = mover.send(src, by_col.at[r], col_to(column(go, 0)))
    pair.append(mover.send(src, by_col.at[r], col_to(column(0, 1))))
    for half in (0, 1):
        at = slots[half]
        for go, come, side in WAYS:
            cross[half, 0, side] = mover.send(own[half], cell(half, at(0, 0)), row_to(at(0, go)))
    yield
    for half in (0, 1):
        at = slots[half]
        for go, come, side in WAYS:
            near[half, side].wait_recv()
            from_slot = at(come, 0)
            far[half, side] = mover.send(
                cell(half, from_slot, side), cell(half, from_slot, side), row_to(at(go, 0))
            )
    for half in (0, 1):
        at = slots[half]
        for _, come, _ in WAYS:
            from_slot = at(come, 0)
            for go, _, side in WAYS:
                cross[half, come, side] = mover.send(
                    cell(half, from_slot), cell(half, from_slot), row_to(at(0, go))
                )
    yield
    further = {}
    for go, come, side in WAYS:
        ring[side].wait_recv()
        rows = pl.ds(side * HALF, HALF)
        from_slot = column(come, 0)
        further[side] = mover.send(
            by_col.at[from_slot, rows, :], by_col.at[from_slot, rows, :], col_to(column(go, 0))
        )
    for _, come, _ in WAYS:
        from_slot = column(come, 0)
        pair.append(mover.send(by_col.at[from_slot], by_col.at[from_slot], col_to(column(0, 1))))

    def pass_on(half, df):
        at = slots[half]
        for go, come, side in WAYS:
            cross[half, df, side].wait_recv()
            from_slot = at(df, come)
            away[half, df, side] = mover.send(
                cell(half, from_slot, side), cell(half, from_slot, side), row_to(at(0, go))
            )

    for half in (0, 1):
        pass_on(half, 0)
    yield
    for half in (0, 1):
        at = slots[half]
        for side in (0, 1):
            far[half, side].wait_recv()
        from_slot = at(2, 0)
        for go, _, side in WAYS:
            cross[half, 2, side] = mover.send(
                cell(half, from_slot), cell(half, from_slot), row_to(at(0, go))
            )
    for side in (0, 1):
        further[side].wait_recv()
    from_slot = column(2, 0)
    pair.append(mover.send(by_col.at[from_slot], by_col.at[from_slot], col_to(column(0, 1))))
    yield
    for df in (3, 1):
        for half in (0, 1):
            pass_on(half, df)
        yield
    for half in (0, 1):
        pass_on(half, 2)
    yield
    for df in (0, 3, 1, 2):
        for half in (0, 1):
            for side in (0, 1):
                away[half, df, side].wait_recv()
    for copy in pair:
        copy.wait_recv()
    mover.drain()


def collect(src_row, src_col, out, land, hold, sems):
    r, c, nr, nc = position()
    mover = Mover(sems)
    row_a, row_b, row_c, row_d, col_a, col_b, col_c = land
    row_t, row_q, row_u, col_q, col_t = hold
    owned = out.shape[1]
    part = owned // 2
    row_to = lambda slot: (r, slot)
    col_to = lambda slot: (slot, c)
    slots = [plane(0), plane(1)]
    lane = lambda side: pl.ds(side * part, part)
    rows = lambda half: pl.ds(half * HALF, HALF)
    first, second, third, fourth = {}, {}, {}, {}
    order = (2, 1, 3, 0)

    pair = []
    for k, dy in enumerate(order):
        pair.append(mover.send(src_col.at[column(dy, 1)], col_a.at[k], col_to(column(0, 1))))
    for k, df in enumerate(order):
        for half in (0, 1):
            at = slots[half]
            for go, come, side in WAYS:
                first[half, k, side] = mover.send(
                    src_row.at[at(df, 2), rows(half), lane(side)], row_a.at[half, k, side],
                    row_to(at(0, go)),
                )
    for k, df in enumerate(order):
        for half in (0, 1):
            at = slots[half]
            for go, come, side in WAYS:
                first[half, k, side].wait_recv()
                keep, other = src_row[at(df, go), rows(half), lane(side)], 1 - side
                row_t[half, k, side, :, lane(side)] = keep + row_a[half, k, side]
                row_t[half, k, side, :, lane(other)] = src_row[at(df, go), rows(half), lane(other)]
                second[half, k, side] = mover.send(
                    row_t.at[half, k, side], row_b.at[half, k, side], row_to(at(0, go))
                )

    for k, dy in enumerate(order):
        pair[k].wait_recv()
        col_q[k] = src_col[column(dy, 0)] + col_a[k]
        if k == 0:
            ring = {}
            for go, come, side in WAYS:
                ring[side] = mover.send(
                    col_q.at[0, rows(side), :], col_b.at[side], col_to(column(go, 0))
                )

    def join(half, k, df):
        at = slots[half]
        for side in (0, 1):
            second[half, k, side].wait_recv()
        row_q[half, k] = (
            src_row[at(df, 0), rows(half), :] + row_b[half, k, 0] + row_b[half, k, 1]
        )

    for half in (0, 1):
        join(half, 0, 2)
        at = slots[half]
        for go, come, side in WAYS:
            third[half, side] = mover.send(
                row_q.at[half, 0, :, lane(side)], row_c.at[half, side], row_to(at(go, 0))
            )
    further = {}
    for go, come, side in WAYS:
        k = order.index(go)
        ring[side].wait_recv()
        other = 1 - side
        col_t[side, rows(side), :] = col_q[k, rows(side), :] + col_b[side]
        col_t[side, rows(other), :] = col_q[k, rows(other), :]
        further[side] = mover.send(col_t.at[side], col_c.at[side], col_to(column(go, 0)))
    for k, df in ((1, 1), (2, 3)):
        for half in (0, 1):
            join(half, k, df)
    for half in (0, 1):
        at = slots[half]
        for go, come, side in WAYS:
            k, other = order.index(go), 1 - side
            third[half, side].wait_recv()
            row_u[half, side, :, lane(side)] = row_q[half, k, :, lane(side)] + row_c[half, side]
            row_u[half, side, :, lane(other)] = row_q[half, k, :, lane(other)]
            fourth[half, side] = mover.send(
                row_u.at[half, side], row_d.at[half, side], row_to(at(go, 0))
            )
    for half in (0, 1):
        join(half, 3, 0)
    for side in (0, 1):
        further[side].wait_recv()
    total = col_q[3] + col_c[0] + col_c[1]
    for half in (0, 1):
        for side in (0, 1):
            fourth[half, side].wait_recv()
        out[rows(half), :] = (
            total[half * HALF:(half + 1) * HALF] + row_q[half, 3] + row_d[half, 0] + row_d[half, 1]
        )
    mover.drain()


def finish(copies):
    for copy in copies:
        copy.wait()


def lanes(x):
    total = x[:, 0:128]
    for k in range(1, x.shape[1] // 128):
        total = total + x[:, k * 128:(k + 1) * 128]
    return total


def reduce_row(mine, land, sems, base):
    r, c, nr, nc = position()
    copies = []
    for o in range(1, nc):
        copies.append(remote(mine, land.at[o - 1], sems, base + o - 1, (r, lax.rem(c + o, nc))))
    for copy in copies:
        copy.start()
    return copies


def reduce_col(mine, land, sems, base):
    r, c, nr, nc = position()
    copies = []
    for o in range(1, nr):
        copies.append(remote(mine, land.at[o - 1], sems, base + o - 1, (lax.rem(r + o, nr), c)))
    for copy in copies:
        copy.start()
    return copies


def total_of(mine, land, n):
    total = mine[...]
    for o in range(n):
        total = total + land[o]
    return total


def tiles_kernel(lists, pts, v, khi, klo, vr, vc, own, pr, pc, psem, vsem):
    r, c, nr, nc = position()
    held = own.shape[0]
    for b in range(held):
        block = pts[:, b * BLK:(b + 1) * BLK]
        own[b] = block
        pr[c * held + b] = block
        pc[r * held + b] = block
    vr[c] = v[...]
    vc[r] = v[...]
    barrier()
    early = []
    for o in range(1, nc):
        to = pr.at[pl.ds(c * held, held)]
        early.append(remote(own, to, psem, len(early), (r, lax.rem(c + o, nc))))
    for o in range(1, nr):
        to = pc.at[pl.ds(r * held, held)]
        early.append(remote(own, to, psem, len(early), (lax.rem(r + o, nr), c)))
    for copy in early:
        copy.start()
    late = spread(v, vr, vc, vsem)
    next(late)
    finish(early)

    def tile(s, _):
        left = pr[lists[0, s]]
        right = pc[lists[1, s]]
        down = jnp.transpose(left)
        for k in range(0, BLK, 32):
            square = None
            for x in range(3):
                offset = down[k:k + 32, x:x + 1] - right[x:x + 1, :]
                square = offset * offset if square is None else square + offset * offset
            scaled = 2.0 * (square * lax.rsqrt(jnp.maximum(square, 1e-30)))
            remain = jnp.maximum(1.0 - scaled, 0.0)
            remain = remain * remain
            value = remain * remain * (4.0 * scaled + 1.0)
            high = value.astype(BF16)
            khi[s, k:k + 32, :] = high
            klo[s, k:k + 32, :] = (value - high.astype(F32)).astype(BF16)
        return 0

    slots, pauses = lists.shape[1], 7
    for k in range(pauses):
        lax.fori_loop(slots * k // pauses, slots * (k + 1) // pauses, tile, 0)
        next(late, None)


def split(x):
    high = x.astype(BF16)
    low = (x - high.astype(F32)).astype(BF16)
    return high, low


def contract(x, khi, klo, dims):
    n = x.shape[0]
    high, low = split(x)
    both = jnp.concatenate([high, low], axis=0)
    first = lax.dot_general(both, khi, (dims, ((), ())), preferred_element_type=F32)
    second = lax.dot_general(high, klo, (dims, ((), ())), preferred_element_type=F32)
    return first[:n] + first[n:] + second


def apply_kernel(lists, khi, klo, vr, vc, sr, sc):
    r, c, nr, nc = position()
    sr[...] = jnp.zeros_like(sr)
    sc[...] = jnp.zeros_like(sc)
    slots = lists.shape[1]
    live = lax.fori_loop(0, slots, lambda s, n: n + lists[2, s], 0)

    def visit(s, _):
        i, j = lists[0, s], lists[1, s]
        di, dj = lax.shift_right_logical(i, 3), lax.shift_right_logical(j, 3)
        bi = pl.ds(pl.multiple_of((i & 7) * BLK, BLK), BLK)
        bj = pl.ds(pl.multiple_of((j & 7) * BLK, BLK), BLK)
        same = jnp.logical_and(jnp.logical_and(di == c, dj == r), (i & 7) == (j & 7))
        mirror = jnp.where(same, 0.0, 1.0).astype(F32)
        high, low = khi[s], klo[s]
        sr[di, :, bi] += contract(vc[dj, :, bj], high, low, ((1,), (1,)))
        sc[dj, :, bj] += mirror * contract(vr[di, :, bi], high, low, ((1,), (0,)))
        return 0

    lax.fori_loop(0, live, visit, 0)


def merge_kernel(d, sr, sc, w, vr, vc, dots, sums, *rest):
    land, hold = rest[:7], rest[7:12]
    mine, land_a, land_b, csem, vsem, dsem = rest[12:]
    r, c, nr, nc = position()
    barrier()
    collect(sr, sc, sums, land, hold, csem)
    image = d[...] + sums[...]
    w[...] = image
    vr[c] = image
    vc[r] = image
    mine[0, 0] = lanes(d[...] * d[...])
    mine[0, 1] = lanes(d[...] * image)
    late = spread(w, vr, vc, vsem)
    next(late)
    first = reduce_row(mine.at[0], land_a, dsem, 0)
    for _ in range(3):
        next(late)
    finish(first)
    mine[1] = total_of(mine.at[0], land_a, nc - 1)
    second = reduce_col(mine.at[1], land_b, dsem, nc - 1)
    for _ in late:
        pass
    finish(second)
    dots[...] = total_of(mine.at[1], land_b, nr - 1)


def final_kernel(d, w, sr, sc, dots, x, res, sums, *rest):
    land, hold = rest[:7], rest[7:12]
    mine, land_a, land_b, csem, dsem = rest[12:]
    r, c, nr, nc = position()
    norm = jnp.sum(dots[0], axis=1, keepdims=True)
    step = norm / jnp.sum(dots[1], axis=1, keepdims=True)
    residual = d[...] - step * w[...]
    mine[0] = lanes(residual * residual)
    barrier()
    first = reduce_row(mine.at[0], land_a, dsem, 0)
    collect(sr, sc, sums, land, hold, csem)
    finish(first)
    mine[1] = total_of(mine.at[0], land_a, nc - 1)
    second = reduce_col(mine.at[1], land_b, dsem, nc - 1)
    finish(second)
    fresh = jnp.sum(total_of(mine.at[1], land_b, nr - 1), axis=1, keepdims=True)
    growth = fresh / norm
    image = w[...] + sums[...]
    direction = residual + growth * d[...]
    applied = w[...] - step * image + growth * w[...]
    mine[2] = lanes(direction * applied)
    third = reduce_row(mine.at[2], land_a.at[pl.ds(nc - 1, nc - 1)], dsem, nc + nr - 2)
    finish(third)
    total = mine[2]
    for o in range(nc - 1):
        total = total + land_a[nc - 1 + o]
    mine[3] = total
    fourth = reduce_col(mine.at[3], land_b.at[pl.ds(nr - 1, nr - 1)], dsem, 2 * nc + nr - 3)
    finish(fourth)
    for o in range(nr - 1):
        total = total + land_b[nr - 1 + o]
    stride = fresh / jnp.sum(total, axis=1, keepdims=True)
    x[...] = step * d[...] + stride * direction
    res[...] = residual - stride * applied


def params(cid=None):
    if cid is None:
        return pltpu.CompilerParams(vmem_limit_bytes=24000 * 1024)
    return pltpu.CompilerParams(collective_id=cid, has_side_effects=True, vmem_limit_bytes=24000 * 1024)


def shape(*dims, dtype=F32):
    return jax.ShapeDtypeStruct(dims, dtype)


def local(points, values, tile_lists):
    nr, nc = lax.axis_size("row"), lax.axis_size("col")
    fields, owned = values.shape
    slots = tile_lists.shape[1]
    peers = nr + nc - 2
    sem = lambda n: pltpu.SemaphoreType.DMA((2, n))
    rows, cols = shape(nc, fields, owned), shape(nr, fields, owned)
    tile = shape(slots, BLK, BLK, dtype=BF16)
    part = owned // 2
    landing = [
        pltpu.VMEM((fields, owned), F32),
        pltpu.VMEM((2, SIDE, 2, HALF, part), F32),
        pltpu.VMEM((2, SIDE, 2, HALF, owned), F32),
        pltpu.VMEM((2, 2, HALF, part), F32),
        pltpu.VMEM((2, 2, HALF, owned), F32),
        pltpu.VMEM((SIDE, fields, owned), F32),
        pltpu.VMEM((2, HALF, owned), F32),
        pltpu.VMEM((2, fields, owned), F32),
        pltpu.VMEM((2, SIDE, 2, HALF, owned), F32),
        pltpu.VMEM((2, SIDE, HALF, owned), F32),
        pltpu.VMEM((2, 2, HALF, owned), F32),
        pltpu.VMEM((SIDE, fields, owned), F32),
        pltpu.VMEM((2, fields, owned), F32),
    ]
    ways = 48

    khi, klo, vr, vc = pl.pallas_call(
        tiles_kernel,
        out_shape=(tile, tile, rows, cols),
        in_specs=[SM, VM, VM],
        out_specs=[VM] * 4,
        scratch_shapes=[
            pltpu.VMEM((owned // BLK, 3, BLK), F32),
            pltpu.VMEM((nc * owned // BLK, 3, BLK), F32),
            pltpu.VMEM((nr * owned // BLK, 3, BLK), F32),
            sem(peers), sem(ways),
        ],
        compiler_params=params(0),
        name="gather_and_tiles",
    )(tile_lists, points, values)

    apply = pl.pallas_call(
        apply_kernel,
        out_shape=(rows, cols),
        in_specs=[SM, VM, VM, VM, VM],
        out_specs=[VM] * 2,
        compiler_params=params(),
        name="apply_tiles",
    )
    sr, sc = apply(tile_lists, khi, klo, vr, vc)

    w, wr, wc, dots = pl.pallas_call(
        merge_kernel,
        out_shape=(shape(fields, owned), rows, cols, shape(2, fields, 128)),
        in_specs=[VM] * 3,
        out_specs=[VM] * 4,
        scratch_shapes=landing + [
            pltpu.VMEM((2, 2, fields, 128), F32),
            pltpu.VMEM((nc - 1, 2, fields, 128), F32),
            pltpu.VMEM((nr - 1, 2, fields, 128), F32),
            sem(ways), sem(ways), sem(peers),
        ],
        compiler_params=params(1),
        name="reduce_and_gather",
    )(values, sr, sc)

    sr, sc = apply(tile_lists, khi, klo, wr, wc)

    x, res = pl.pallas_call(
        final_kernel,
        out_shape=(shape(fields, owned), shape(fields, owned)),
        in_specs=[VM] * 5,
        out_specs=[VM] * 2,
        scratch_shapes=landing + [
            pltpu.VMEM((4, fields, 128), F32),
            pltpu.VMEM((2 * (nc - 1), fields, 128), F32),
            pltpu.VMEM((2 * (nr - 1), fields, 128), F32),
            sem(ways), sem(2 * peers),
        ],
        compiler_params=params(2),
        name="reduce_and_finish",
    )(values, w, sr, sc, dots)
    return x, res


def solution(mesh):
    placed = P(None, ("row", "col"))
    return jax.shard_map(
        local, mesh=mesh, in_specs=(placed,) * 3, out_specs=(placed, placed), check_vma=False
    )
```

profile of v0, /device:TPU:1, one launch (start us, length us, event | category | flops | bytes accessed | tf_op | source)
XLA Modules:
  0.0 140.3 jit_solution(14605878815072625458)
XLA Ops:
  0.6 0.0 copy-start
  0.6 0.9 copy-done
  1.5 0.0 copy-start.2
  1.5 0.8 copy-done.2
  2.3 0.0 copy-start.3
  2.3 0.7 copy-done.3
  3.0 37.5 %gather_and_tiles.1 = (bf16[48,256,256]{2,1,0:T(8,128)(2,1)S(1)}, bf16[48,256,256]{2,1,0:T(8,128)(2,1)S(1)}, f32[16,16,2048]{2,1,0:T(8,128)S(1)}, f32[8,16,2048]{2,1,0:T(8,128)S(1)}) custom-call(s32[3,48]{1,0:T(4,128)S(1)} %copy-done.3, f32[3,2048]{1,0:T(4,128)S(1)} %copy-done.2, f32[16,2048]{1,0:T(8,128)S(1)} %copy-done), custom_call_target="tpu_custom_call" | custom-call | tf_op jit(solution)/shard_map/gather_and_tiles/pallas_call | solution.py:497
  40.5 5.9 %apply_tiles.2 = (f32[16,16,2048]{2,1,0:T(8,128)S(1)}, f32[8,16,2048]{2,1,0:T(8,128)S(1)}) custom-call(s32[3,48]{1,0:T(4,128)S(1)} %copy-done.3, bf16[48,256,256]{2,1,0:T(8,128)(2,1)S(1)} %get-tuple-element.14.khi, bf16[48,256,256]{2,1,0:T(8,128)(2,1)S(1)} %get-tuple-element.15.klo, f32[16,16,2048]{2,1,0:T(8,128)S(1)} %get-tuple-element.16.vr, ...), custom_call_target="tpu_custom_call" | custom-call | tf_op jit(solution)/shard_map/apply_tiles/pallas_call | solution.py:520
  46.4 44.1 %reduce_and_gather.1 = (f32[16,2048]{1,0:T(8,128)S(1)}, f32[16,16,2048]{2,1,0:T(8,128)S(1)}, f32[8,16,2048]{2,1,0:T(8,128)S(1)}, f32[2,16,128]{2,1,0:T(8,128)S(1)}) custom-call(f32[16,2048]{1,0:T(8,128)S(1)} %copy-done, f32[16,16,2048]{2,1,0:T(8,128)S(1)} %get-tuple-element.18.sr, f32[8,16,2048]{2,1,0:T(8,128)S(1)} %get-tuple-element.19.sc), custom_call_target="tpu_custom_call" | custom-call | tf_op jit(solution)/shard_map/reduce_and_gather/pallas_call | solution.py:522
  90.4 0.0 copy-start.1
  90.5 5.9 %apply_tiles.3 = (f32[16,16,2048]{2,1,0:T(8,128)S(1)}, f32[8,16,2048]{2,1,0:T(8,128)S(1)}) custom-call(s32[3,48]{1,0:T(4,128)S(1)} %copy-done.3, bf16[48,256,256]{2,1,0:T(8,128)(2,1)S(1)} %get-tuple-element.14.khi, bf16[48,256,256]{2,1,0:T(8,128)(2,1)S(1)} %get-tuple-element.15.klo, f32[16,16,2048]{2,1,0:T(8,128)S(1)} %get-tuple-element.21.vr, ...), custom_call_target="tpu_custom_call" | custom-call | tf_op jit(solution)/shard_map/apply_tiles/pallas_call | solution.py:537
  96.3 0.0 copy-done.1
  96.3 42.6 %reduce_and_finish.1 = (f32[16,2048]{1,0:T(8,128)S(1)}, f32[16,2048]{1,0:T(8,128)S(1)}) custom-call(f32[16,2048]{1,0:T(8,128)S(1)} %copy-done.1, f32[16,2048]{1,0:T(8,128)S(1)} %get-tuple-element.20.w, f32[16,16,2048]{2,1,0:T(8,128)S(1)} %get-tuple-element.23.sr, f32[8,16,2048]{2,1,0:T(8,128)S(1)} %get-tuple-element.24.sc, ...), custom_call_target="tpu_custom_call" | custom-call | tf_op jit(solution)/shard_map/reduce_and_finish/pallas_call | solution.py:539
  138.9 0.7 copy.7
  139.6 0.7 copy.8
Async XLA Ops:
  0.6 0.9 copy-start
  1.5 0.8 copy-start.2
  2.3 0.7 copy-start.3
  90.4 5.9 %copy-start.1 = (f32[16,2048]{1,0:T(8,128)S(1)}, f32[16,2048]{1,0:T(8,128)}, u32[]{:S(2)}) copy-start(f32[16,2048]{1,0:T(8,128)} %d.3) | copy-start | bytes 393220
where the time goes:
time: 140 us
  Pallas kernels  136 us (97%)
  local copies, waits for them, and re-layouts  3.66 us (3%)
    pallas_call x1, Pallas kernels, local(): pl.pallas_call(merge_kernel, out_shape=(shape(fields, owned), rows, cols,...  44.1 us
    pallas_call x1, Pallas kernels, local(): pl.pallas_call(final_kernel, out_shape=(shape(fields, owned), shape(field...  42.6 us
    pallas_call x1, Pallas kernels, local(): pl.pallas_call(tiles_kernel, out_shape=(tile, tile, rows, cols), in_specs...  37.5 us
    pallas_call x1, Pallas kernels, local(): sr, sc = apply(tile_lists, khi, klo, wr, wc)  5.88 us
    pallas_call x1, Pallas kernels, local(): sr, sc = apply(tile_lists, khi, klo, vr, vc)  5.87 us
    unnamed x10, local copies, waits for them, and re-layouts  3.66 us

commit v1 on v0

--- a/solution.py
+++ b/solution.py
@@ -200,6 +200,7 @@
                     src_row.at[at(df, 2), rows(half), lane(side)], row_a.at[half, k, side],
                     row_to(at(0, go)),
                 )
+    yield
     for k, df in enumerate(order):
         for half in (0, 1):
             at = slots[half]
@@ -237,6 +238,7 @@
             third[half, side] = mover.send(
                 row_q.at[half, 0, :, lane(side)], row_c.at[half, side], row_to(at(go, 0))
             )
+    yield
     further = {}
     for go, come, side in WAYS:
         k = order.index(go)
@@ -258,6 +260,7 @@
             fourth[half, side] = mover.send(
                 row_u.at[half, side], row_d.at[half, side], row_to(at(go, 0))
             )
+    yield
     for half in (0, 1):
         join(half, 3, 0)
     for side in (0, 1):
@@ -401,7 +404,8 @@
     mine, land_a, land_b, csem, vsem, dsem = rest[12:]
     r, c, nr, nc = position()
     barrier()
-    collect(sr, sc, sums, land, hold, csem)
+    for _ in collect(sr, sc, sums, land, hold, csem):
+        pass
     image = d[...] + sums[...]
     w[...] = image
     vr[c] = image
@@ -422,38 +426,63 @@
     dots[...] = total_of(mine.at[1], land_b, nr - 1)
 
 
-def final_kernel(d, w, sr, sc, dots, x, res, sums, *rest):
+def local_dots(sr, sc, vr, vc, wr, wc, step):
+    fields = sr.shape[1]
+    size = 256
+
+    def over(part, dirs, images, n, carry):
+        pieces = part.shape[2] // size
+
+        def body(k, carry):
+            with_residual, with_direction = carry
+            for p in range(pieces):
+                cut = slice(p * size, (p + 1) * size)
+                direction, image = dirs[k, :, cut], images[k, :, cut]
+                product = part[k, :, cut]
+                with_residual = with_residual + lanes(product * (direction - step * image))
+                with_direction = with_direction + lanes(product * direction)
+            return with_residual, with_direction
+
+        return lax.fori_loop(0, n, body, carry)
+
+    zero = jnp.zeros((fields, 128), F32)
+    carry = over(sr, vr, wr, sr.shape[0], (zero, zero))
+    return over(sc, vc, wc, sc.shape[0], carry)
+
+
+def final_kernel(d, w, sr, sc, dots, vr, vc, wr, wc, x, res, sums, *rest):
     land, hold = rest[:7], rest[7:12]
     mine, land_a, land_b, csem, dsem = rest[12:]
     r, c, nr, nc = position()
     norm = jnp.sum(dots[0], axis=1, keepdims=True)
-    step = norm / jnp.sum(dots[1], axis=1, keepdims=True)
+    cross = jnp.sum(dots[1], axis=1, keepdims=True)
+    step = norm / cross
     residual = d[...] - step * w[...]
-    mine[0] = lanes(residual * residual)
     barrier()
+    parts = collect(sr, sc, sums, land, hold, csem)
+    next(parts)
+    with_residual, with_direction = local_dots(sr, sc, vr, vc, wr, wc, step)
+    along = lanes(residual * w[...])
+    mine[0, 0] = lanes(residual * residual)
+    mine[0, 1] = along - step * (along + with_residual)
+    mine[0, 2] = along - step * with_direction
     first = reduce_row(mine.at[0], land_a, dsem, 0)
-    collect(sr, sc, sums, land, hold, csem)
+    next(parts)
     finish(first)
     mine[1] = total_of(mine.at[0], land_a, nc - 1)
     second = reduce_col(mine.at[1], land_b, dsem, nc - 1)
+    for _ in parts:
+        pass
     finish(second)
-    fresh = jnp.sum(total_of(mine.at[1], land_b, nr - 1), axis=1, keepdims=True)
+    totals = total_of(mine.at[1], land_b, nr - 1)
+    fresh = jnp.sum(totals[0], axis=1, keepdims=True)
     growth = fresh / norm
+    square = jnp.sum(totals[1], axis=1, keepdims=True)
+    mixed = jnp.sum(totals[2], axis=1, keepdims=True) + (cross - step * cross)
+    stride = fresh / (square + growth * mixed + growth * growth * cross)
     image = w[...] + sums[...]
     direction = residual + growth * d[...]
     applied = w[...] - step * image + growth * w[...]
-    mine[2] = lanes(direction * applied)
-    third = reduce_row(mine.at[2], land_a.at[pl.ds(nc - 1, nc - 1)], dsem, nc + nr - 2)
-    finish(third)
-    total = mine[2]
-    for o in range(nc - 1):
-        total = total + land_a[nc - 1 + o]
-    mine[3] = total
-    fourth = reduce_col(mine.at[3], land_b.at[pl.ds(nr - 1, nr - 1)], dsem, 2 * nc + nr - 3)
-    finish(fourth)
-    for o in range(nr - 1):
-        total = total + land_b[nr - 1 + o]
-    stride = fresh / jnp.sum(total, axis=1, keepdims=True)
     x[...] = step * d[...] + stride * direction
     res[...] = residual - stride * applied
 
@@ -539,17 +568,17 @@
     x, res = pl.pallas_call(
         final_kernel,
         out_shape=(shape(fields, owned), shape(fields, owned)),
-        in_specs=[VM] * 5,
+        in_specs=[VM] * 9,
         out_specs=[VM] * 2,
         scratch_shapes=landing + [
-            pltpu.VMEM((4, fields, 128), F32),
-            pltpu.VMEM((2 * (nc - 1), fields, 128), F32),
-            pltpu.VMEM((2 * (nr - 1), fields, 128), F32),
-            sem(ways), sem(2 * peers),
+            pltpu.VMEM((2, 3, fields, 128), F32),
+            pltpu.VMEM((nc - 1, 3, fields, 128), F32),
+            pltpu.VMEM((nr - 1, 3, fields, 128), F32),
+            sem(ways), sem(peers),
         ],
         compiler_params=params(2),
         name="reduce_and_finish",
-    )(values, w, sr, sc, dots)
+    )(values, w, sr, sc, dots, vr, vc, wr, wc)
     return x, res
 
 

time: 140 us -> 124 us (0.89)
  Pallas kernels: 136 us -> 119 us
    pallas_call x1, Pallas kernels: 42.6 us -> 28.2 us  [local(): pl.pallas_call(final_kernel, out_shape=(shape(fields, owned), shape(field...]
    pallas_call x1, Pallas kernels: 44.1 us -> 39.9 us  [local(): pl.pallas_call(merge_kernel, out_shape=(shape(fields, owned), rows, cols,...]
where the time goes in v1:
time: 124 us; the launch traced here: 123 us
  Pallas kernels  119 us (96%)
  local copies, waits for them, and re-layouts  3.66 us (3%)
    pallas_call x1, Pallas kernels, local(): pl.pallas_call(merge_kernel, out_shape=(shape(fields, owned), rows, cols,...  39.9 us
    pallas_call x1, Pallas kernels, local(): pl.pallas_call(tiles_kernel, out_shape=(tile, tile, rows, cols), in_specs...  37.5 us
    pallas_call x1, Pallas kernels, local(): pl.pallas_call(final_kernel, out_shape=(shape(fields, owned), shape(field...  28.2 us
    pallas_call x1, Pallas kernels, local(): sr, sc = apply(tile_lists, khi, klo, vr, vc)  6.65 us
    pallas_call x1, Pallas kernels, local(): sr, sc = apply(tile_lists, khi, klo, wr, wc)  6.65 us
    unnamed x10, local copies, waits for them, and re-layouts  3.66 us

profile of v1, /device:TPU:1, one launch (start us, length us, event | category | flops | bytes accessed | tf_op | source)
XLA Modules:
  0.0 123.3 jit_solution(14106622948779740039)
XLA Ops:
  0.6 0.0 copy-start
  0.6 0.9 copy-done
  1.5 0.0 copy-start.2
  1.5 0.8 copy-done.2
  2.3 0.0 copy-start.3
  2.3 0.7 copy-done.3
  3.0 37.5 %gather_and_tiles.1 = (bf16[48,256,256]{2,1,0:T(8,128)(2,1)S(1)}, bf16[48,256,256]{2,1,0:T(8,128)(2,1)S(1)}, f32[16,16,2048]{2,1,0:T(8,128)S(1)}, f32[8,16,2048]{2,1,0:T(8,128)S(1)}) custom-call(s32[3,48]{1,0:T(4,128)S(1)} %copy-done.3, f32[3,2048]{1,0:T(4,128)S(1)} %copy-done.2, f32[16,2048]{1,0:T(8,128)S(1)} %copy-done), custom_call_target="tpu_custom_call" | custom-call | tf_op jit(solution)/shard_map/gather_and_tiles/pallas_call | solution.py:526
  40.5 0.0 copy-start.1
  40.5 6.6 %apply_tiles.2 = (f32[16,16,2048]{2,1,0:T(8,128)S(1)}, f32[8,16,2048]{2,1,0:T(8,128)S(1)}) custom-call(s32[3,48]{1,0:T(4,128)S(1)} %copy-done.3, bf16[48,256,256]{2,1,0:T(8,128)(2,1)S(1)} %get-tuple-element.14.khi, bf16[48,256,256]{2,1,0:T(8,128)(2,1)S(1)} %get-tuple-element.15.klo, f32[16,16,2048]{2,1,0:T(8,128)S(1)} %get-tuple-element.16.vr, ...), custom_call_target="tpu_custom_call" | custom-call | tf_op jit(solution)/shard_map/apply_tiles/pallas_call | solution.py:549
  47.1 0.0 copy-done.1
  47.1 39.9 %reduce_and_gather.1 = (f32[16,2048]{1,0:T(8,128)S(1)}, f32[16,16,2048]{2,1,0:T(8,128)S(1)}, f32[8,16,2048]{2,1,0:T(8,128)S(1)}, f32[2,16,128]{2,1,0:T(8,128)S(1)}) custom-call(f32[16,2048]{1,0:T(8,128)S(1)} %copy-done.1, f32[16,16,2048]{2,1,0:T(8,128)S(1)} %get-tuple-element.18.sr, f32[8,16,2048]{2,1,0:T(8,128)S(1)} %get-tuple-element.19.sc), custom_call_target="tpu_custom_call" | custom-call | tf_op jit(solution)/shard_map/reduce_and_gather/pallas_call | solution.py:551
  87.1 6.6 %apply_tiles.3 = (f32[16,16,2048]{2,1,0:T(8,128)S(1)}, f32[8,16,2048]{2,1,0:T(8,128)S(1)}) custom-call(s32[3,48]{1,0:T(4,128)S(1)} %copy-done.3, bf16[48,256,256]{2,1,0:T(8,128)(2,1)S(1)} %get-tuple-element.14.khi, bf16[48,256,256]{2,1,0:T(8,128)(2,1)S(1)} %get-tuple-element.15.klo, f32[16,16,2048]{2,1,0:T(8,128)S(1)} %get-tuple-element.21.vr.wr, ...), custom_call_target="tpu_custom_call" | custom-call | tf_op jit(solution)/shard_map/apply_tiles/pallas_call | solution.py:566
  93.7 28.2 %reduce_and_finish.1 = (f32[16,2048]{1,0:T(8,128)S(1)}, f32[16,2048]{1,0:T(8,128)S(1)}) custom-call(f32[16,2048]{1,0:T(8,128)S(1)} %copy-done.1, f32[16,2048]{1,0:T(8,128)S(1)} %get-tuple-element.20.w, f32[16,16,2048]{2,1,0:T(8,128)S(1)} %get-tuple-element.23.sr, f32[8,16,2048]{2,1,0:T(8,128)S(1)} %get-tuple-element.24.sc, ...), custom_call_target="tpu_custom_call" | custom-call | tf_op jit(solution)/shard_map/reduce_and_finish/pallas_call | solution.py:568
  122.0 0.7 copy.7
  122.6 0.7 copy.8
Async XLA Ops:
  0.6 0.9 copy-start
  1.5 0.8 copy-start.2
  2.3 0.7 copy-start.3
  40.5 6.7 %copy-start.1 = (f32[16,2048]{1,0:T(8,128)S(1)}, f32[16,2048]{1,0:T(8,128)}, u32[]{:S(2)}) copy-start(f32[16,2048]{1,0:T(8,128)} %d.3) | copy-start | bytes 393220

commit v2 on v1

--- a/solution.py
+++ b/solution.py
@@ -318,7 +318,7 @@
     r, c, nr, nc = position()
     held = own.shape[0]
     for b in range(held):
-        block = pts[:, b * BLK:(b + 1) * BLK]
+        block = 2.0 * pts[:, b * BLK:(b + 1) * BLK]
         own[b] = block
         pr[c * held + b] = block
         pc[r * held + b] = block
@@ -347,7 +347,7 @@
             for x in range(3):
                 offset = down[k:k + 32, x:x + 1] - right[x:x + 1, :]
                 square = offset * offset if square is None else square + offset * offset
-            scaled = 2.0 * (square * lax.rsqrt(jnp.maximum(square, 1e-30)))
+            scaled = square * lax.rsqrt(jnp.maximum(square, 1e-30))
             remain = jnp.maximum(1.0 - scaled, 0.0)
             remain = remain * remain
             value = remain * remain * (4.0 * scaled + 1.0)
@@ -384,19 +384,29 @@
     slots = lists.shape[1]
     live = lax.fori_loop(0, slots, lambda s, n: n + lists[2, s], 0)
 
-    def visit(s, _):
-        i, j = lists[0, s], lists[1, s]
-        di, dj = lax.shift_right_logical(i, 3), lax.shift_right_logical(j, 3)
-        bi = pl.ds(pl.multiple_of((i & 7) * BLK, BLK), BLK)
-        bj = pl.ds(pl.multiple_of((j & 7) * BLK, BLK), BLK)
-        same = jnp.logical_and(jnp.logical_and(di == c, dj == r), (i & 7) == (j & 7))
-        mirror = jnp.where(same, 0.0, 1.0).astype(F32)
-        high, low = khi[s], klo[s]
-        sr[di, :, bi] += contract(vc[dj, :, bj], high, low, ((1,), (1,)))
-        sc[dj, :, bj] += mirror * contract(vr[di, :, bi], high, low, ((1,), (0,)))
+    together = 4 if slots % 4 == 0 else 1
+
+    def visit(g, _):
+        updates = []
+        for k in range(together):
+            s = g * together + k
+            i, j = lists[0, s], lists[1, s]
+            di, dj = lax.shift_right_logical(i, 3), lax.shift_right_logical(j, 3)
+            bi = pl.ds(pl.multiple_of((i & 7) * BLK, BLK), BLK)
+            bj = pl.ds(pl.multiple_of((j & 7) * BLK, BLK), BLK)
+            same = jnp.logical_and(jnp.logical_and(di == c, dj == r), (i & 7) == (j & 7))
+            weight = lists[2, s].astype(F32)
+            mirror = jnp.where(same, 0.0, weight).astype(F32)
+            high, low = khi[s], klo[s]
+            ahead = weight * contract(vc[dj, :, bj], high, low, ((1,), (1,)))
+            behind = mirror * contract(vr[di, :, bi], high, low, ((1,), (0,)))
+            updates.append((di, bi, ahead, dj, bj, behind))
+        for di, bi, ahead, dj, bj, behind in updates:
+            sr[di, :, bi] += ahead
+            sc[dj, :, bj] += behind
         return 0
 
-    lax.fori_loop(0, live, visit, 0)
+    lax.fori_loop(0, lax.div(live + together - 1, together), visit, 0)
 
 
 def merge_kernel(d, sr, sc, w, vr, vc, dots, sums, *rest):

time: 124 us -> 119 us (0.960)
  Pallas kernels: 119 us -> 113 us
    pallas_call x1, Pallas kernels: 6.65 us -> 4.27 us  [local(): sr, sc = apply(tile_lists, khi, klo, vr, vc)]
    pallas_call x1, Pallas kernels: 6.65 us -> 4.27 us  [local(): sr, sc = apply(tile_lists, khi, klo, wr, wc)]
where the time goes in v2:
time: 119 us; the launch traced here: 117 us
  Pallas kernels  113 us (95%)
  local copies, waits for them, and re-layouts  3.66 us (3%)
    pallas_call x1, Pallas kernels, local(): pl.pallas_call(merge_kernel, out_shape=(shape(fields, owned), rows, cols,...  39.4 us
    pallas_call x1, Pallas kernels, local(): pl.pallas_call(tiles_kernel, out_shape=(tile, tile, rows, cols), in_specs...  37.2 us
    pallas_call x1, Pallas kernels, local(): pl.pallas_call(final_kernel, out_shape=(shape(fields, owned), shape(field...  27.8 us
    pallas_call x1, Pallas kernels, local(): sr, sc = apply(tile_lists, khi, klo, vr, vc)  4.27 us
    pallas_call x1, Pallas kernels, local(): sr, sc = apply(tile_lists, khi, klo, wr, wc)  4.27 us
    unnamed x10, local copies, waits for them, and re-layouts  3.66 us

profile of v2, /device:TPU:1, one launch (start us, length us, event | category | flops | bytes accessed | tf_op | source)
XLA Modules:
  0.0 117.3 jit_solution(179785975023036511)
XLA Ops:
  0.6 0.0 copy-start
  0.6 0.9 copy-done
  1.5 0.0 copy-start.2
  1.5 0.8 copy-done.2
  2.3 0.0 copy-start.3
  2.3 0.7 copy-done.3
  3.0 37.2 %gather_and_tiles.1 = (bf16[48,256,256]{2,1,0:T(8,128)(2,1)S(1)}, bf16[48,256,256]{2,1,0:T(8,128)(2,1)S(1)}, f32[16,16,2048]{2,1,0:T(8,128)S(1)}, f32[8,16,2048]{2,1,0:T(8,128)S(1)}) custom-call(s32[3,48]{1,0:T(4,128)S(1)} %copy-done.3, f32[3,2048]{1,0:T(4,128)S(1)} %copy-done.2, f32[16,2048]{1,0:T(8,128)S(1)} %copy-done), custom_call_target="tpu_custom_call" | custom-call | tf_op jit(solution)/shard_map/gather_and_tiles/pallas_call | solution.py:536
  40.2 0.0 copy-start.1
  40.2 4.3 %apply_tiles.2 = (f32[16,16,2048]{2,1,0:T(8,128)S(1)}, f32[8,16,2048]{2,1,0:T(8,128)S(1)}) custom-call(s32[3,48]{1,0:T(4,128)S(1)} %copy-done.3, bf16[48,256,256]{2,1,0:T(8,128)(2,1)S(1)} %get-tuple-element.14.khi, bf16[48,256,256]{2,1,0:T(8,128)(2,1)S(1)} %get-tuple-element.15.klo, f32[16,16,2048]{2,1,0:T(8,128)S(1)} %get-tuple-element.16.vr, ...), custom_call_target="tpu_custom_call" | custom-call | tf_op jit(solution)/shard_map/apply_tiles/pallas_call | solution.py:559
  44.5 0.0 copy-done.1
  44.5 39.4 %reduce_and_gather.1 = (f32[16,2048]{1,0:T(8,128)S(1)}, f32[16,16,2048]{2,1,0:T(8,128)S(1)}, f32[8,16,2048]{2,1,0:T(8,128)S(1)}, f32[2,16,128]{2,1,0:T(8,128)S(1)}) custom-call(f32[16,2048]{1,0:T(8,128)S(1)} %copy-done.1, f32[16,16,2048]{2,1,0:T(8,128)S(1)} %get-tuple-element.18.sr, f32[8,16,2048]{2,1,0:T(8,128)S(1)} %get-tuple-element.19.sc), custom_call_target="tpu_custom_call" | custom-call | tf_op jit(solution)/shard_map/reduce_and_gather/pallas_call | solution.py:561
  83.9 4.3 %apply_tiles.3 = (f32[16,16,2048]{2,1,0:T(8,128)S(1)}, f32[8,16,2048]{2,1,0:T(8,128)S(1)}) custom-call(s32[3,48]{1,0:T(4,128)S(1)} %copy-done.3, bf16[48,256,256]{2,1,0:T(8,128)(2,1)S(1)} %get-tuple-element.14.khi, bf16[48,256,256]{2,1,0:T(8,128)(2,1)S(1)} %get-tuple-element.15.klo, f32[16,16,2048]{2,1,0:T(8,128)S(1)} %get-tuple-element.21.vr.wr, ...), custom_call_target="tpu_custom_call" | custom-call | tf_op jit(solution)/shard_map/apply_tiles/pallas_call | solution.py:576
  88.2 27.8 %reduce_and_finish.1 = (f32[16,2048]{1,0:T(8,128)S(1)}, f32[16,2048]{1,0:T(8,128)S(1)}) custom-call(f32[16,2048]{1,0:T(8,128)S(1)} %copy-done.1, f32[16,2048]{1,0:T(8,128)S(1)} %get-tuple-element.20.w, f32[16,16,2048]{2,1,0:T(8,128)S(1)} %get-tuple-element.23.sr, f32[8,16,2048]{2,1,0:T(8,128)S(1)} %get-tuple-element.24.sc, ...), custom_call_target="tpu_custom_call" | custom-call | tf_op jit(solution)/shard_map/reduce_and_finish/pallas_call | solution.py:578
  116.0 0.7 copy.7
  116.6 0.7 copy.8
Async XLA Ops:
  0.6 0.9 copy-start
  1.5 0.8 copy-start.2
  2.3 0.7 copy-start.3
  40.2 4.3 %copy-start.1 = (f32[16,2048]{1,0:T(8,128)S(1)}, f32[16,2048]{1,0:T(8,128)}, u32[]{:S(2)}) copy-start(f32[16,2048]{1,0:T(8,128)} %d.3) | copy-start | bytes 393220

commit v3 on v2

--- a/solution.py
+++ b/solution.py
@@ -409,31 +409,43 @@
     lax.fori_loop(0, lax.div(live + together - 1, together), visit, 0)
 
 
-def merge_kernel(d, sr, sc, w, vr, vc, dots, sums, *rest):
+def local_dot(sr, sc, dr, dc):
+    fields = sr.shape[1]
+
+    def over(part, vectors, carry):
+        body = lambda k, total: total + lanes(part[k] * vectors[k])
+        return lax.fori_loop(0, part.shape[0], body, carry)
+
+    return over(sc, dc, over(sr, dr, jnp.zeros((fields, 128), F32)))
+
+
+def merge_kernel(d, sr, sc, dr, dc, w, vr, vc, dots, sums, *rest):
     land, hold = rest[:7], rest[7:12]
     mine, land_a, land_b, csem, vsem, dsem = rest[12:]
     r, c, nr, nc = position()
     barrier()
-    for _ in collect(sr, sc, sums, land, hold, csem):
+    parts = collect(sr, sc, sums, land, hold, csem)
+    next(parts)
+    square = lanes(d[...] * d[...])
+    mine[0, 0] = square
+    mine[0, 1] = square + local_dot(sr, sc, dr, dc)
+    first = reduce_row(mine.at[0], land_a, dsem, 0)
+    next(parts)
+    finish(first)
+    mine[1] = total_of(mine.at[0], land_a, nc - 1)
+    second = reduce_col(mine.at[1], land_b, dsem, nc - 1)
+    for _ in parts:
         pass
     image = d[...] + sums[...]
     w[...] = image
     vr[c] = image
     vc[r] = image
-    mine[0, 0] = lanes(d[...] * d[...])
-    mine[0, 1] = lanes(d[...] * image)
     late = spread(w, vr, vc, vsem)
     next(late)
-    first = reduce_row(mine.at[0], land_a, dsem, 0)
-    for _ in range(3):
-        next(late)
-    finish(first)
-    mine[1] = total_of(mine.at[0], land_a, nc - 1)
-    second = reduce_col(mine.at[1], land_b, dsem, nc - 1)
+    finish(second)
+    dots[...] = total_of(mine.at[1], land_b, nr - 1)
     for _ in late:
         pass
-    finish(second)
-    dots[...] = total_of(mine.at[1], land_b, nr - 1)
 
 
 def local_dots(sr, sc, vr, vc, wr, wc, step):
@@ -561,7 +573,7 @@
     w, wr, wc, dots = pl.pallas_call(
         merge_kernel,
         out_shape=(shape(fields, owned), rows, cols, shape(2, fields, 128)),
-        in_specs=[VM] * 3,
+        in_specs=[VM] * 5,
         out_specs=[VM] * 4,
         scratch_shapes=landing + [
             pltpu.VMEM((2, 2, fields, 128), F32),
@@ -571,7 +583,7 @@
         ],
         compiler_params=params(1),
         name="reduce_and_gather",
-    )(values, sr, sc)
+    )(values, sr, sc, vr, vc)
 
     sr, sc = apply(tile_lists, khi, klo, wr, wc)
 

time: 119 us -> 118 us (level); the launches traced: 117 us -> 118 us
    unnamed x10 -> x8, local copies, waits for them, and re-layouts: 3.66 us -> 3.65 us
where the time goes in v3:
time: 118 us
  Pallas kernels  113 us (96%)
  local copies, waits for them, and re-layouts  3.65 us (3%)
    pallas_call x1, Pallas kernels, local(): pl.pallas_call(merge_kernel, out_shape=(shape(fields, owned), rows, cols,...  39.3 us
    pallas_call x1, Pallas kernels, local(): pl.pallas_call(tiles_kernel, out_shape=(tile, tile, rows, cols), in_specs...  37.2 us
    pallas_call x1, Pallas kernels, local(): pl.pallas_call(final_kernel, out_shape=(shape(fields, owned), shape(field...  27.1 us
    pallas_call x1, Pallas kernels, local(): sr, sc = apply(tile_lists, khi, klo, vr, vc)  4.81 us
    pallas_call x1, Pallas kernels, local(): sr, sc = apply(tile_lists, khi, klo, wr, wc)  4.81 us
    unnamed x8, local copies, waits for them, and re-layouts  3.65 us

profile of v3, /device:TPU:1, one launch (start us, length us, event | category | flops | bytes accessed | tf_op | source)
XLA Modules:
  0.0 117.6 jit_solution(12727637333403652388)
XLA Ops:
  0.6 0.0 copy-start
  0.6 0.9 copy-done
  1.5 0.0 copy-start.1
  1.5 0.8 copy-done.1
  2.3 0.0 copy-start.2
  2.3 0.7 copy-done.2
  3.0 37.2 %gather_and_tiles.1 = (bf16[48,256,256]{2,1,0:T(8,128)(2,1)S(1)}, bf16[48,256,256]{2,1,0:T(8,128)(2,1)S(1)}, f32[16,16,2048]{2,1,0:T(8,128)S(1)}, f32[8,16,2048]{2,1,0:T(8,128)S(1)}) custom-call(s32[3,48]{1,0:T(4,128)S(1)} %copy-done.2, f32[3,2048]{1,0:T(4,128)S(1)} %copy-done.1, f32[16,2048]{1,0:T(8,128)S(1)} %copy-done), custom_call_target="tpu_custom_call" | custom-call | tf_op jit(solution)/shard_map/gather_and_tiles/pallas_call | solution.py:548
  40.2 4.8 %apply_tiles.2 = (f32[16,16,2048]{2,1,0:T(8,128)S(1)}, f32[8,16,2048]{2,1,0:T(8,128)S(1)}) custom-call(s32[3,48]{1,0:T(4,128)S(1)} %copy-done.2, bf16[48,256,256]{2,1,0:T(8,128)(2,1)S(1)} %get-tuple-element.14.khi, bf16[48,256,256]{2,1,0:T(8,128)(2,1)S(1)} %get-tuple-element.15.klo, f32[16,16,2048]{2,1,0:T(8,128)S(1)} %get-tuple-element.16.vr.dr, ...), custom_call_target="tpu_custom_call" | custom-call | tf_op jit(solution)/shard_map/apply_tiles/pallas_call | solution.py:571
  45.0 39.3 %reduce_and_gather.1 = (f32[16,2048]{1,0:T(8,128)S(1)}, f32[16,16,2048]{2,1,0:T(8,128)S(1)}, f32[8,16,2048]{2,1,0:T(8,128)S(1)}, f32[2,16,128]{2,1,0:T(8,128)S(1)}) custom-call(f32[16,2048]{1,0:T(8,128)S(1)} %copy-done, f32[16,16,2048]{2,1,0:T(8,128)S(1)} %get-tuple-element.18.sr, f32[8,16,2048]{2,1,0:T(8,128)S(1)} %get-tuple-element.19.sc, ...), custom_call_target="tpu_custom_call" | custom-call | tf_op jit(solution)/shard_map/reduce_and_gather/pallas_call | solution.py:573
  84.3 4.8 %apply_tiles.3 = (f32[16,16,2048]{2,1,0:T(8,128)S(1)}, f32[8,16,2048]{2,1,0:T(8,128)S(1)}) custom-call(s32[3,48]{1,0:T(4,128)S(1)} %copy-done.2, bf16[48,256,256]{2,1,0:T(8,128)(2,1)S(1)} %get-tuple-element.14.khi, bf16[48,256,256]{2,1,0:T(8,128)(2,1)S(1)} %get-tuple-element.15.klo, f32[16,16,2048]{2,1,0:T(8,128)S(1)} %get-tuple-element.21.vr.wr, ...), custom_call_target="tpu_custom_call" | custom-call | tf_op jit(solution)/shard_map/apply_tiles/pallas_call | solution.py:588
  89.1 27.1 %reduce_and_finish.1 = (f32[16,2048]{1,0:T(8,128)S(1)}, f32[16,2048]{1,0:T(8,128)S(1)}) custom-call(f32[16,2048]{1,0:T(8,128)S(1)} %copy-done, f32[16,2048]{1,0:T(8,128)S(1)} %get-tuple-element.20.w, f32[16,16,2048]{2,1,0:T(8,128)S(1)} %get-tuple-element.23.sr, f32[8,16,2048]{2,1,0:T(8,128)S(1)} %get-tuple-element.24.sc, ...), custom_call_target="tpu_custom_call" | custom-call | tf_op jit(solution)/shard_map/reduce_and_finish/pallas_call | solution.py:590
  116.3 0.7 copy.7
  116.9 0.7 copy.8
Async XLA Ops:
  0.6 0.9 copy-start
  1.5 0.8 copy-start.1
  2.3 0.7 copy-start.2

commit v4 on v3

--- a/solution.py
+++ b/solution.py
@@ -356,10 +356,12 @@
             klo[s, k:k + 32, :] = (value - high.astype(F32)).astype(BF16)
         return 0
 
-    slots, pauses = lists.shape[1], 7
+    slots, pauses = lists.shape[1], 6
     for k in range(pauses):
+        next(late)
         lax.fori_loop(slots * k // pauses, slots * (k + 1) // pauses, tile, 0)
-        next(late, None)
+    for _ in late:
+        pass
 
 
 def split(x):

time: 118 us -> 117 us (level); the launches traced: 118 us -> 115 us
  Pallas kernels: 113 us -> 111 us
    pallas_call x1, Pallas kernels: 39.3 us -> 36.9 us  [local(): pl.pallas_call(merge_kernel, out_shape=(shape(fields, owned), rows, cols,...]
where the time goes in v4:
time: 117 us; the launch traced here: 115 us
  Pallas kernels  111 us (95%)
  local copies, waits for them, and re-layouts  3.65 us (3%)
    pallas_call x1, Pallas kernels, local(): pl.pallas_call(tiles_kernel, out_shape=(tile, tile, rows, cols), in_specs...  37.5 us
    pallas_call x1, Pallas kernels, local(): pl.pallas_call(merge_kernel, out_shape=(shape(fields, owned), rows, cols,...  36.9 us
    pallas_call x1, Pallas kernels, local(): pl.pallas_call(final_kernel, out_shape=(shape(fields, owned), shape(field...  27.8 us
    pallas_call x1, Pallas kernels, local(): sr, sc = apply(tile_lists, khi, klo, vr, vc)  4.27 us
    pallas_call x1, Pallas kernels, local(): sr, sc = apply(tile_lists, khi, klo, wr, wc)  4.27 us
    unnamed x8, local copies, waits for them, and re-layouts  3.65 us

profile of v4, /device:TPU:1, one launch (start us, length us, event | category | flops | bytes accessed | tf_op | source)
XLA Modules:
  0.0 115.0 jit_solution(3372422095815431520)
XLA Ops:
  0.6 0.0 copy-start
  0.6 0.9 copy-done
  1.5 0.0 copy-start.1
  1.5 0.8 copy-done.1
  2.3 0.0 copy-start.2
  2.3 0.7 copy-done.2
  3.0 37.5 %gather_and_tiles.1 = (bf16[48,256,256]{2,1,0:T(8,128)(2,1)S(1)}, bf16[48,256,256]{2,1,0:T(8,128)(2,1)S(1)}, f32[16,16,2048]{2,1,0:T(8,128)S(1)}, f32[8,16,2048]{2,1,0:T(8,128)S(1)}) custom-call(s32[3,48]{1,0:T(4,128)S(1)} %copy-done.2, f32[3,2048]{1,0:T(4,128)S(1)} %copy-done.1, f32[16,2048]{1,0:T(8,128)S(1)} %copy-done), custom_call_target="tpu_custom_call" | custom-call | tf_op jit(solution)/shard_map/gather_and_tiles/pallas_call | solution.py:550
  40.5 4.3 %apply_tiles.2 = (f32[16,16,2048]{2,1,0:T(8,128)S(1)}, f32[8,16,2048]{2,1,0:T(8,128)S(1)}) custom-call(s32[3,48]{1,0:T(4,128)S(1)} %copy-done.2, bf16[48,256,256]{2,1,0:T(8,128)(2,1)S(1)} %get-tuple-element.14.khi, bf16[48,256,256]{2,1,0:T(8,128)(2,1)S(1)} %get-tuple-element.15.klo, f32[16,16,2048]{2,1,0:T(8,128)S(1)} %get-tuple-element.16.vr.dr, ...), custom_call_target="tpu_custom_call" | custom-call | tf_op jit(solution)/shard_map/apply_tiles/pallas_call | solution.py:573
  44.8 36.9 %reduce_and_gather.1 = (f32[16,2048]{1,0:T(8,128)S(1)}, f32[16,16,2048]{2,1,0:T(8,128)S(1)}, f32[8,16,2048]{2,1,0:T(8,128)S(1)}, f32[2,16,128]{2,1,0:T(8,128)S(1)}) custom-call(f32[16,2048]{1,0:T(8,128)S(1)} %copy-done, f32[16,16,2048]{2,1,0:T(8,128)S(1)} %get-tuple-element.18.sr, f32[8,16,2048]{2,1,0:T(8,128)S(1)} %get-tuple-element.19.sc, ...), custom_call_target="tpu_custom_call" | custom-call | tf_op jit(solution)/shard_map/reduce_and_gather/pallas_call | solution.py:575
  81.7 4.3 %apply_tiles.3 = (f32[16,16,2048]{2,1,0:T(8,128)S(1)}, f32[8,16,2048]{2,1,0:T(8,128)S(1)}) custom-call(s32[3,48]{1,0:T(4,128)S(1)} %copy-done.2, bf16[48,256,256]{2,1,0:T(8,128)(2,1)S(1)} %get-tuple-element.14.khi, bf16[48,256,256]{2,1,0:T(8,128)(2,1)S(1)} %get-tuple-element.15.klo, f32[16,16,2048]{2,1,0:T(8,128)S(1)} %get-tuple-element.21.vr.wr, ...), custom_call_target="tpu_custom_call" | custom-call | tf_op jit(solution)/shard_map/apply_tiles/pallas_call | solution.py:590
  85.9 27.8 %reduce_and_finish.1 = (f32[16,2048]{1,0:T(8,128)S(1)}, f32[16,2048]{1,0:T(8,128)S(1)}) custom-call(f32[16,2048]{1,0:T(8,128)S(1)} %copy-done, f32[16,2048]{1,0:T(8,128)S(1)} %get-tuple-element.20.w, f32[16,16,2048]{2,1,0:T(8,128)S(1)} %get-tuple-element.23.sr, f32[8,16,2048]{2,1,0:T(8,128)S(1)} %get-tuple-element.24.sc, ...), custom_call_target="tpu_custom_call" | custom-call | tf_op jit(solution)/shard_map/reduce_and_finish/pallas_call | solution.py:592
  113.7 0.7 copy.7
  114.4 0.7 copy.8
Async XLA Ops:
  0.6 0.9 copy-start
  1.5 0.8 copy-start.1
  2.3 0.7 copy-start.2
